TPU v7x, 32 devices: a whole 2x2x4 slice. The times are simulated.
32 devices in a mesh: expert: 4 (over x, core), hidden: 8 (over z, y).
Axes of the slice: x: 2, y: 2, z: 4, core: 2. Of those that a mesh axis runs over, the one named last changes fastest.
Arguments:
- tokens: bfloat16 [128, 6144], P(('expert', 'hidden')), may hold values from -33 to 33
- norm_gain: float32 [6144], replicated, may hold values from 0.1 to 1.9
- gate_weight: bfloat16 [4, 6144, 8192], P('expert', None, 'hidden'), may hold values from -0.078125 to 0.078125
- up_weight: bfloat16 [4, 6144, 8192], P('expert', None, 'hidden'), may hold values from -0.078125 to 0.078125
- down_weight: bfloat16 [4, 8192, 6144], P('expert', 'hidden'), may hold values from -0.09375 to 0.09375
- expert_ids: int32 [128, 2], P('expert'), may hold values from 0 to 3, all different within a row; in each aligned block of 4 rows (0 to 3, 4 to 7, ...) at most 2 rows name the same one
- route_weight: float32 [128, 2], P('expert'), may hold values from 0.2 to 1
Outputs:
- settled_state: bfloat16 [128, 6144], P(('expert', 'hidden'))
Inputs may be any that keep to these rules, and one draw needn't show every extreme that they name: `expert_ids`: in each aligned block of 4 rows (the tokens of one device) the two ids of a row differ and no expert is named more than 2 times; some expert is named exactly 2 times.
All inputs are finite; a program needn't handle non-finite values.
Results may differ from a plain program's by a relative error of at most 0.0085.
Values may be sent and summed in bfloat16 or wider, within the bound.
A program may use at most 64 MiB of HBM per device.

v0:
```python
import jax
import jax.numpy as jnp
from jax import lax
from jax.sharding import PartitionSpec as P

ITERS = 2
EPSILON = 1e-05
NUDGE = 0.5


def rms_norm(values, norm_gain):
    widened = values.astype(jnp.float32)
    mean_square = jnp.mean(widened * widened, axis=-1, keepdims=True)
    return (widened * lax.rsqrt(mean_square + EPSILON) * norm_gain).astype(jnp.bfloat16)


def slot_table(id_blocks, experts, capacity):
    groups = id_blocks.shape[0]
    tok_count = id_blocks.shape[1]
    flat_ids = id_blocks.reshape(groups, tok_count * 2)
    expert_range = jnp.arange(experts, dtype=jnp.int32)
    one_hot = (flat_ids[:, :, None] == expert_range[None, None, :]).astype(jnp.int32)
    before = jnp.cumsum(one_hot, axis=1) - one_hot
    within = jnp.sum(before * one_hot, axis=2)
    return (flat_ids * capacity + within).reshape(groups, tok_count, 2)


def dispatch(token_block, slots, slot_count):
    groups = token_block.shape[0]
    tok_count = token_block.shape[1]
    width = token_block.shape[2]
    token_index = jnp.broadcast_to(
        jnp.arange(tok_count, dtype=jnp.int32)[None, :, None], slots.shape
    )
    group_index = jnp.broadcast_to(jnp.arange(groups, dtype=jnp.int32)[:, None, None], slots.shape)
    source = (
        jnp.full((groups, slot_count), tok_count, jnp.int32).at[group_index, slots].set(token_index)
    )
    padded = jnp.concatenate(
        [token_block, jnp.zeros((groups, 1, width), token_block.dtype)], axis=1
    )
    return jax.vmap(lambda table_rows, chosen: jnp.take(table_rows, chosen, axis=0))(padded, source)


def expert_partial(inputs, gate_weight, up_weight, down_weight):
    gate_value = jnp.dot(inputs, gate_weight[0], preferred_element_type=jnp.float32)
    up_value = jnp.dot(inputs, up_weight[0], preferred_element_type=jnp.float32)
    hidden_units = (jax.nn.silu(gate_value) * up_value).astype(jnp.bfloat16)
    return jnp.dot(hidden_units, down_weight[0], preferred_element_type=jnp.float32)


def on_device(tokens, norm_gain, gate_weight, up_weight, down_weight, expert_ids, route_weight):
    experts = lax.axis_size("expert")
    tok_count = tokens.shape[0]
    capacity = tok_count // 2
    slot_count = experts * capacity
    position = lax.axis_index("hidden")
    own_ids = lax.dynamic_slice_in_dim(expert_ids, position * tok_count, tok_count, 0)
    own_weights = lax.dynamic_slice_in_dim(route_weight, position * tok_count, tok_count, 0)
    own_slots = slot_table(own_ids[None], experts, capacity)[0]
    state = tokens
    for iteration in range(ITERS):
        normed = rms_norm(state, norm_gain)
        outgoing = dispatch(normed[None], own_slots[None], slot_count)[0]
        arrived = lax.all_to_all(outgoing, "expert", split_axis=0, concat_axis=0, tiled=True)
        gathered = lax.all_gather(arrived, "hidden", axis=0, tiled=True)
        partials = expert_partial(gathered, gate_weight, up_weight, down_weight)
        summed = lax.psum_scatter(
            partials.astype(jnp.bfloat16), "hidden", scatter_dimension=0, tiled=True
        )
        returned = lax.all_to_all(summed, "expert", split_axis=0, concat_axis=0, tiled=True)
        first = (
            jnp.take(returned, own_slots[:, 0], axis=0).astype(jnp.float32) * own_weights[:, 0:1]
        )
        second = (
            jnp.take(returned, own_slots[:, 1], axis=0).astype(jnp.float32) * own_weights[:, 1:2]
        )
        mixed = first + second
        state = (
            NUDGE * state.astype(jnp.float32) + NUDGE * (tokens.astype(jnp.float32) + mixed)
        ).astype(jnp.bfloat16)
    return state


def solution(mesh):
    placed = (
        P(("expert", "hidden"), None),
        P(),
        P("expert", None, "hidden"),
        P("expert", None, "hidden"),
        P("expert", "hidden", None),
        P("expert", None),
        P("expert", None),
    )
    return jax.shard_map(
        on_device,
        mesh=mesh,
        in_specs=placed,
        out_specs=P(("expert", "hidden"), None),
        check_vma=False,
    )
```

profile of v0, /device:TPU:0, one launch (start us, length us, event | category | flops | bytes accessed | tf_op | source)
XLA Modules:
  0.0 285.9 jit_solution(7350800166975226673)
XLA Ops:
  6.5 0.0 copy-start
  6.5 0.0 reduce-scatter.3.cloned.1.call-start
  6.5 0.7 copy-done
  7.2 0.1 constant_dynamic-slice_fusion.1
  7.3 0.1 copy.20
  7.4 0.1 eq.27
  7.5 0.2 reduce_window_sum.11
  7.7 0.1 reduce_sum.31
  7.8 0.1 copy.17
  7.9 0.1 copy.19
  8.0 0.1 reshape.240
  8.1 0.1 reshape.242
  8.2 0.6 scatter_custom_fusion
  8.8 1.0 fusion.51
  9.8 0.9 fusion.56
  10.7 0.8 gather_fusion
  11.6 0.1 bitcast_select_fusion.1
  11.7 0.1 all_to_all.32
  11.7 8.3 %all_to_all.48 = bf16[4,2,6144]{2,1,0:T(2,128)(2,1)S(1)} all-to-all(bf16[4,2,6144]{2,1,0:T(2,128)(2,1)S(1)} %all_to_all.32), channel_id=1, replica_groups=mesh['expert'=4,'hidden'=8] {'expert'}, dimensions={0} | all-to-all | bytes 196608 | tf_op jit(solution)/shard_map/all_to_all | solution.py:65
  20.1 32.4 %all_gather.6 = bf16[64,6144]{1,0:T(8,128)(2,1)S(1)} all-gather(bf16[8,6144]{1,0:T(8,128)(2,1)S(1)} %all_to_all.34), channel_id=1, replica_groups=mesh['expert'=4,'hidden'=8] {'hidden'}, dimensions={0}, use_global_device_ids=true | all-gather | bytes 884736 | tf_op jit(solution)/shard_map/all_gather | solution.py:66
  52.5 6.9 %fusion.10 = f32[64,1024]{1,0:T(8,128)S(1)} fusion(bf16[64,6144]{1,0:T(8,128)(2,1)S(1)} %all_gather.6, bf16[1,6144,1024]{2,1,0:T(8,128)(2,1)} %param.13), kind=kOutput, calls=%fused_computation.17 | convolution fusion | flops 805306368 | bytes 13631488 | tf_op jit(solution)/shard_map/dot_general | solution.py:46
  59.4 0.0 copy-start.3
  59.4 0.0 copy-start.1
  59.4 0.0 copy-start.2
  59.5 13.6 %fusion.12 = bf16[64,6144]{1,0:T(8,128)(2,1)} fusion(bf16[1,1024,6144]{2,1,0:T(8,128)(2,1)} %param.15, bf16[64,6144]{1,0:T(8,128)(2,1)S(1)} %all_gather.6, bf16[1,6144,1024]{2,1,0:T(8,128)(2,1)} %param.14, f32[64,1024]{1,0:T(8,128)S(1)} %fusion.10), kind=kOutput, calls=%fused_computation.19 | convolution fusion | flops 1611399168 | bytes 27000832 | tf_op jit(solution)/shard_map/dot_general | solution.py:49
  73.0 0.0 reduce-scatter.3.cloned.1.call-update
  73.1 0.0 copy-done.3
  73.1 0.1 constant_dynamic-slice_fusion
  73.2 0.2 slice_reduce_fusion.1
  73.4 63.1 %reduce-scatter.3.cloned.1.call-done = bf16[8,6144]{1,0:T(8,128)(2,1)} async-done(((bf16[64,6144]{1,0:T(8,128)(2,1)}), bf16[8,6144]{1,0:T(8,128)(2,1)}) %reduce-scatter.3.cloned.1.call-update) | async-done | bytes 98320 | tf_op jit(solution)/shard_map/reduce_scatter | solution.py:68
  136.5 1.6 all_to_all.35
  138.1 3.3 %all-to-all-start.1 = ((bf16[4,2,6144]{2,1,0:T(2,128)(2,1)}), bf16[4,2,6144]{2,1,0:T(2,128)(2,1)S(1)}, u32[]{:S(2)}, u32[]{:S(2)}) async-start(bf16[4,2,6144]{2,1,0:T(2,128)(2,1)} %all_to_all.35), calls=%async_computation.2 | async-start | bytes 196608 | tf_op jit(solution)/shard_map/all_to_all | solution.py:71
  141.4 0.0 reduce-scatter.5.cloned.1.call-start
  141.5 4.2 %all-to-all-done.1 = bf16[4,2,6144]{2,1,0:T(2,128)(2,1)S(1)} async-done(((bf16[4,2,6144]{2,1,0:T(2,128)(2,1)}), bf16[4,2,6144]{2,1,0:T(2,128)(2,1)S(1)}, u32[]{:S(2)}, u32[]{:S(2)}) %all-to-all-start.1) | async-done | bytes 98336 | tf_op jit(solution)/shard_map/all_to_all | solution.py:71
  145.7 0.6 gather_fusion.2
  146.3 0.6 gather_fusion.1
  146.9 0.0 copy-done.1
  146.9 0.3 fusion.46
  147.2 0.0 copy-done.2
  147.2 0.1 fusion.57
  147.3 0.8 gather_fusion.3
  148.2 0.1 bitcast_select_fusion
  148.3 0.1 all_to_all.38
  148.3 6.7 %all_to_all.49 = bf16[4,2,6144]{2,1,0:T(2,128)(2,1)S(1)} all-to-all(bf16[4,2,6144]{2,1,0:T(2,128)(2,1)S(1)} %all_to_all.38), channel_id=1, replica_groups=mesh['expert'=4,'hidden'=8] {'expert'}, dimensions={0} | all-to-all | bytes 196608 | tf_op jit(solution)/shard_map/all_to_all | solution.py:65
  155.1 32.3 %all_gather.7 = bf16[64,6144]{1,0:T(8,128)(2,1)S(1)} all-gather(bf16[8,6144]{1,0:T(8,128)(2,1)S(1)} %all_to_all.40), channel_id=1, replica_groups=mesh['expert'=4,'hidden'=8] {'hidden'}, dimensions={0}, use_global_device_ids=true | all-gather | bytes 884736 | tf_op jit(solution)/shard_map/all_gather | solution.py:66
  187.3 6.9 %fusion.8 = f32[64,1024]{1,0:T(8,128)S(1)} fusion(bf16[64,6144]{1,0:T(8,128)(2,1)S(1)} %all_gather.7, bf16[1,6144,1024]{2,1,0:T(8,128)(2,1)} %param.13), kind=kOutput, calls=%fused_computation.15 | convolution fusion | flops 805306368 | bytes 13631488 | tf_op jit(solution)/shard_map/dot_general | solution.py:46
  194.2 13.6 %fusion.15 = bf16[64,6144]{1,0:T(8,128)(2,1)} fusion(bf16[1,1024,6144]{2,1,0:T(8,128)(2,1)} %param.15, bf16[64,6144]{1,0:T(8,128)(2,1)S(1)} %all_gather.7, bf16[1,6144,1024]{2,1,0:T(8,128)(2,1)} %param.14, f32[64,1024]{1,0:T(8,128)S(1)} %fusion.8), kind=kOutput, calls=%fused_computation.20 | convolution fusion | flops 1611399168 | bytes 27000832 | tf_op jit(solution)/shard_map/dot_general | solution.py:49
  207.8 0.0 reduce-scatter.5.cloned.1.call-update
  207.8 61.5 %reduce-scatter.5.cloned.1.call-done = bf16[8,6144]{1,0:T(8,128)(2,1)} async-done(((bf16[64,6144]{1,0:T(8,128)(2,1)}), bf16[8,6144]{1,0:T(8,128)(2,1)}) %reduce-scatter.5.cloned.1.call-update) | async-done | bytes 98320 | tf_op jit(solution)/shard_map/reduce_scatter | solution.py:68
  269.3 1.0 all_to_all.41
  270.3 6.8 %all_to_all.50 = bf16[4,2,6144]{2,1,0:T(2,128)(2,1)S(1)} all-to-all(bf16[4,2,6144]{2,1,0:T(2,128)(2,1)S(1)} %all_to_all.41), channel_id=1, replica_groups=mesh['expert'=4,'hidden'=8] {'expert'}, dimensions={0} | all-to-all | bytes 196608 | tf_op jit(solution)/shard_map/all_to_all | solution.py:71
  277.1 0.6 gather_fusion.5
  277.7 0.6 gather_fusion.4
  278.3 0.8 fusion.50
  (23 shorter events, 0.3 us)
Async XLA Ops:
  6.5 0.7 copy-start
  6.5 130.0 %reduce-scatter.3.cloned.1.call-start = ((), (), s32[]{:S(2)}) async-start(), calls=%async_computation.6 | async-start | bytes 884736 | tf_op jit(solution)/shard_map/reduce_scatter | solution.py:68
  59.4 13.7 %copy-start.3 = (f32[32,2]{0,1:T(2,128)S(1)}, f32[32,2]{0,1:T(2,128)}, u32[]{:S(2)}) copy-start(f32[32,2]{0,1:T(2,128)} %param.17) | copy-start | bytes 772
  59.4 87.5 %copy-start.1 = (bf16[4,6144]{1,0:T(4,128)(2,1)S(1)}, bf16[4,6144]{1,0:T(4,128)(2,1)}, u32[]{:S(2)}) copy-start(bf16[4,6144]{1,0:T(4,128)(2,1)} %param.11) | copy-start | bytes 147460
  59.4 87.8 %copy-start.2 = (f32[6144]{0:T(1024)S(1)}, f32[6144]{0:T(1024)}, u32[]{:S(2)}) copy-start(f32[6144]{0:T(1024)} %param.12) | copy-start | bytes 73732
  138.1 7.6 %all-to-all-start.1 = ((bf16[4,2,6144]{2,1,0:T(2,128)(2,1)}), bf16[4,2,6144]{2,1,0:T(2,128)(2,1)S(1)}, u32[]{:S(2)}, u32[]{:S(2)}) async-start(bf16[4,2,6144]{2,1,0:T(2,128)(2,1)} %all_to_all.35), calls=%async_computation.2 | async-start | bytes 196608 | tf_op jit(solution)/shard_map/all_to_all | solution.py:71
  141.4 127.9 %reduce-scatter.5.cloned.1.call-start = ((), (), s32[]{:S(2)}) async-start(), calls=%async_computation.7 | async-start | bytes 884736 | tf_op jit(solution)/shard_map/reduce_scatter | solution.py:68
Sparse Core Ops, SparseCore 0:
  73.2 63.2 reduce-scatter.2
  207.9 61.2 reduce-scatter.4
where the time goes:
time: 286 us
  waiting for transfers between devices  129 us (45%)
  blocking collectives  86.4 us (30%)
  matrix products  40.9 us (14%)
  between operations  13.6 us (5%)
  local copies, waits for them, and re-layouts  9.26 us (3%)
  other arithmetic  3.46 us (1%)
  starting transfers between devices  3.35 us (1%)
    reduce_scatter x2, waiting for transfers between devices, on_device(): lax.psum_scatter(partials.astype(jnp.bfloat16), 'hidden', scatter_dimensi...  125 us
    all_gather x2, blocking collectives, on_device(): gathered = lax.all_gather(arrived, 'hidden', axis=0, tiled=True)  64.7 us
    dot_general x2, matrix products, expert_partial(): jnp.dot(hidden_units, down_weight[0], preferred_element_type=jnp.float32)  27.2 us
    all_to_all x2, blocking collectives, on_device(): lax.all_to_all(outgoing, 'expert', split_axis=0, concat_axis=0, tiled=True)  15 us
    dot_general x2, matrix products, expert_partial(): jnp.dot(inputs, gate_weight[0], preferred_element_type=jnp.float32)  13.8 us
    all_to_all x1, blocking collectives, on_device(): lax.all_to_all(summed, 'expert', split_axis=0, concat_axis=0, tiled=True)  6.77 us
  transfers between devices with their start and end apart: 3, of which 3 were waited for; matrix products, arithmetic and copies ran while one was open for 0% of the time, Pallas kernels for 0%

commit v1 on v0

--- a/solution.py
+++ b/solution.py
@@ -1,11 +1,24 @@
+import functools
 import jax
 import jax.numpy as jnp
 from jax import lax
 from jax.sharding import PartitionSpec as P
+from jax.lax import all_to_all, axis_size
 
 ITERS = 2
 EPSILON = 1e-05
 NUDGE = 0.5
+
+
+def load_the_cells(original, mesh_dim, array_axis):
+    now = all_to_all(
+        jnp.stack(axis_size(mesh_dim) * [original]), axis_name=mesh_dim, split_axis=0, concat_axis=0
+    )
+    then = jnp.concatenate(now, axis=array_axis)
+    return then
+
+
+connect_goods = functools.partial(load_the_cells, mesh_dim="hidden", array_axis=0)
 
 
 def rms_norm(values, norm_gain):
@@ -63,7 +76,7 @@
         normed = rms_norm(state, norm_gain)
         outgoing = dispatch(normed[None], own_slots[None], slot_count)[0]
         arrived = lax.all_to_all(outgoing, "expert", split_axis=0, concat_axis=0, tiled=True)
-        gathered = lax.all_gather(arrived, "hidden", axis=0, tiled=True)
+        gathered = connect_goods(arrived)
         partials = expert_partial(gathered, gate_weight, up_weight, down_weight)
         summed = lax.psum_scatter(
             partials.astype(jnp.bfloat16), "hidden", scatter_dimension=0, tiled=True

time: 286 us -> 269 us (0.941)
  blocking collectives: 86.4 us -> 70.6 us
    all_gather x2 -> x0, blocking collectives: 64.7 us -> none  [on_device(): gathered = lax.all_gather(arrived, 'hidden', axis=0, tiled=True)]
    all_to_all x0 -> x2, blocking collectives: none -> 48.7 us  [load_the_cells(): all_to_all(jnp.stack(axis_size(mesh_dim) * [original]), axis_name=mesh_di...]
where the time goes in v1:
time: 269 us
  waiting for transfers between devices  127 us (47%)
  blocking collectives  70.6 us (26%)
  matrix products  40.9 us (15%)
  between operations  13.6 us (5%)
  local copies, waits for them, and re-layouts  9.36 us (3%)
  other arithmetic  3.46 us (1%)
  starting transfers between devices  3.35 us (1%)
    reduce_scatter x2, waiting for transfers between devices, on_device(): lax.psum_scatter(partials.astype(jnp.bfloat16), 'hidden', scatter_dimensi...  123 us
    all_to_all x2, blocking collectives, load_the_cells(): all_to_all(jnp.stack(axis_size(mesh_dim) * [original]), axis_name=mesh_di...  48.7 us
    dot_general x2, matrix products, expert_partial(): jnp.dot(hidden_units, down_weight[0], preferred_element_type=jnp.float32)  27.2 us
    all_to_all x2, blocking collectives, on_device(): lax.all_to_all(outgoing, 'expert', split_axis=0, concat_axis=0, tiled=True)  15 us
    dot_general x2, matrix products, expert_partial(): jnp.dot(inputs, gate_weight[0], preferred_element_type=jnp.float32)  13.8 us
    all_to_all x1, blocking collectives, on_device(): lax.all_to_all(summed, 'expert', split_axis=0, concat_axis=0, tiled=True)  6.84 us
  transfers between devices with their start and end apart: 3, of which 3 were waited for; matrix products, arithmetic and copies ran while one was open for 0% of the time, Pallas kernels for 0%

profile of v1, /device:TPU:0, one launch (start us, length us, event | category | flops | bytes accessed | tf_op | source)
XLA Modules:
  0.0 268.5 jit_solution(3975840039827679754)
XLA Ops:
  6.5 0.0 copy-start
  6.5 0.0 reduce-scatter.3.cloned.1.call-start
  6.5 0.7 copy-done
  7.2 0.1 constant_dynamic-slice_fusion.1
  7.3 0.1 copy.20
  7.4 0.1 eq.27
  7.5 0.2 reduce_window_sum.11
  7.7 0.1 reduce_sum.31
  7.8 0.1 copy.17
  7.9 0.1 copy.19
  8.0 0.1 reshape.254
  8.1 0.1 reshape.256
  8.2 0.6 scatter_custom_fusion
  8.8 1.0 fusion.59
  9.8 0.9 fusion.64
  10.7 0.8 gather_fusion
  11.6 0.1 bitcast_select_fusion.1
  11.7 0.1 all_to_all.34
  11.7 8.3 %all_to_all.52 = bf16[4,2,6144]{2,1,0:T(2,128)(2,1)S(1)} all-to-all(bf16[4,2,6144]{2,1,0:T(2,128)(2,1)S(1)} %all_to_all.34), channel_id=1, replica_groups=mesh['expert'=4,'hidden'=8] {'expert'}, dimensions={0} | all-to-all | bytes 196608 | tf_op jit(solution)/shard_map/all_to_all | solution.py:78
  20.1 0.1 stack.9
  20.2 25.5 %all_to_all.53 = bf16[8,8,6144]{2,1,0:T(8,128)(2,1)S(1)} all-to-all(bf16[8,8,6144]{2,1,0:T(8,128)(2,1)S(1)} %stack.9), channel_id=1, replica_groups=mesh['expert'=4,'hidden'=8] {'hidden'}, dimensions={0} | all-to-all | bytes 1572864 | tf_op jit(solution)/shard_map/all_to_all | solution.py:14
  45.7 6.9 %fusion.10 = f32[64,1024]{1,0:T(8,128)S(1)} fusion(bf16[1,6144,1024]{2,1,0:T(8,128)(2,1)} %param.13, bf16[8,8,6144]{2,1,0:T(8,128)(2,1)S(1)} %all_to_all.53), kind=kOutput, calls=%fused_computation.17 | convolution fusion | flops 805306368 | bytes 13631488 | tf_op jit(solution)/shard_map/dot_general | solution.py:59
  52.6 0.0 copy-start.3
  52.6 0.0 copy-start.1
  52.6 0.0 copy-start.2
  52.6 13.6 %fusion.12 = bf16[64,6144]{1,0:T(8,128)(2,1)} fusion(bf16[1,1024,6144]{2,1,0:T(8,128)(2,1)} %param.15, bf16[1,6144,1024]{2,1,0:T(8,128)(2,1)} %param.14, bf16[8,8,6144]{2,1,0:T(8,128)(2,1)S(1)} %all_to_all.53, f32[64,1024]{1,0:T(8,128)S(1)} %fusion.10), kind=kOutput, calls=%fused_computation.19 | convolution fusion | flops 1611399168 | bytes 27000832 | tf_op jit(solution)/shard_map/dot_general | solution.py:62
  66.2 0.0 reduce-scatter.3.cloned.1.call-update
  66.2 0.0 copy-done.3
  66.2 0.1 constant_dynamic-slice_fusion
  66.3 0.2 slice_reduce_fusion.1
  66.5 61.3 %reduce-scatter.3.cloned.1.call-done = bf16[8,6144]{1,0:T(8,128)(2,1)} async-done(((bf16[64,6144]{1,0:T(8,128)(2,1)}), bf16[8,6144]{1,0:T(8,128)(2,1)}) %reduce-scatter.3.cloned.1.call-update) | async-done | bytes 98320 | tf_op jit(solution)/shard_map/reduce_scatter | solution.py:81
  127.9 1.6 all_to_all.37
  129.5 3.3 %all-to-all-start.2 = ((bf16[4,2,6144]{2,1,0:T(2,128)(2,1)}), bf16[4,2,6144]{2,1,0:T(2,128)(2,1)S(1)}, u32[]{:S(2)}, u32[]{:S(2)}) async-start(bf16[4,2,6144]{2,1,0:T(2,128)(2,1)} %all_to_all.37), calls=%async_computation.3 | async-start | bytes 196608 | tf_op jit(solution)/shard_map/all_to_all | solution.py:84
  132.8 0.0 reduce-scatter.5.cloned.1.call-start
  132.9 4.2 %all-to-all-done.2 = bf16[4,2,6144]{2,1,0:T(2,128)(2,1)S(1)} async-done(((bf16[4,2,6144]{2,1,0:T(2,128)(2,1)}), bf16[4,2,6144]{2,1,0:T(2,128)(2,1)S(1)}, u32[]{:S(2)}, u32[]{:S(2)}) %all-to-all-start.2) | async-done | bytes 98336 | tf_op jit(solution)/shard_map/all_to_all | solution.py:84
  137.1 0.6 gather_fusion.2
  137.7 0.6 gather_fusion.1
  138.3 0.0 copy-done.1
  138.3 0.3 fusion.54
  138.6 0.0 copy-done.2
  138.6 0.1 fusion.65
  138.7 0.8 gather_fusion.3
  139.6 0.1 bitcast_select_fusion
  139.7 0.1 all_to_all.40
  139.7 6.7 %all_to_all.54 = bf16[4,2,6144]{2,1,0:T(2,128)(2,1)S(1)} all-to-all(bf16[4,2,6144]{2,1,0:T(2,128)(2,1)S(1)} %all_to_all.40), channel_id=1, replica_groups=mesh['expert'=4,'hidden'=8] {'expert'}, dimensions={0} | all-to-all | bytes 196608 | tf_op jit(solution)/shard_map/all_to_all | solution.py:78
  146.5 0.1 stack.11
  146.5 23.2 %all_to_all.55 = bf16[8,8,6144]{2,1,0:T(8,128)(2,1)S(1)} all-to-all(bf16[8,8,6144]{2,1,0:T(8,128)(2,1)S(1)} %stack.11), channel_id=1, replica_groups=mesh['expert'=4,'hidden'=8] {'hidden'}, dimensions={0} | all-to-all | bytes 1572864 | tf_op jit(solution)/shard_map/all_to_all | solution.py:14
  169.7 6.9 %fusion.8 = f32[64,1024]{1,0:T(8,128)S(1)} fusion(bf16[1,6144,1024]{2,1,0:T(8,128)(2,1)} %param.13, bf16[8,8,6144]{2,1,0:T(8,128)(2,1)S(1)} %all_to_all.55), kind=kOutput, calls=%fused_computation.15 | convolution fusion | flops 805306368 | bytes 13631488 | tf_op jit(solution)/shard_map/dot_general | solution.py:59
  176.6 13.6 %fusion.15 = bf16[64,6144]{1,0:T(8,128)(2,1)} fusion(bf16[1,1024,6144]{2,1,0:T(8,128)(2,1)} %param.15, bf16[1,6144,1024]{2,1,0:T(8,128)(2,1)} %param.14, bf16[8,8,6144]{2,1,0:T(8,128)(2,1)S(1)} %all_to_all.55, f32[64,1024]{1,0:T(8,128)S(1)} %fusion.8), kind=kOutput, calls=%fused_computation.20 | convolution fusion | flops 1611399168 | bytes 27000832 | tf_op jit(solution)/shard_map/dot_general | solution.py:62
  190.2 0.0 reduce-scatter.5.cloned.1.call-update
  190.2 61.6 %reduce-scatter.5.cloned.1.call-done = bf16[8,6144]{1,0:T(8,128)(2,1)} async-done(((bf16[64,6144]{1,0:T(8,128)(2,1)}), bf16[8,6144]{1,0:T(8,128)(2,1)}) %reduce-scatter.5.cloned.1.call-update) | async-done | bytes 98320 | tf_op jit(solution)/shard_map/reduce_scatter | solution.py:81
  251.9 1.0 all_to_all.43
  252.8 6.8 %all_to_all.56 = bf16[4,2,6144]{2,1,0:T(2,128)(2,1)S(1)} all-to-all(bf16[4,2,6144]{2,1,0:T(2,128)(2,1)S(1)} %all_to_all.43), channel_id=1, replica_groups=mesh['expert'=4,'hidden'=8] {'expert'}, dimensions={0} | all-to-all | bytes 196608 | tf_op jit(solution)/shard_map/all_to_all | solution.py:84
  259.7 0.6 gather_fusion.5
  260.3 0.6 gather_fusion.4
  260.9 0.8 fusion.58
  (23 shorter events, 0.3 us)
Async XLA Ops:
  6.5 0.7 copy-start
  6.5 121.3 %reduce-scatter.3.cloned.1.call-start = ((), (), s32[]{:S(2)}) async-start(), calls=%async_computation.8 | async-start | bytes 884736 | tf_op jit(solution)/shard_map/reduce_scatter | solution.py:81
  52.6 13.7 %copy-start.3 = (f32[32,2]{0,1:T(2,128)S(1)}, f32[32,2]{0,1:T(2,128)}, u32[]{:S(2)}) copy-start(f32[32,2]{0,1:T(2,128)} %param.17) | copy-start | bytes 772
  52.6 85.7 %copy-start.1 = (bf16[4,6144]{1,0:T(4,128)(2,1)S(1)}, bf16[4,6144]{1,0:T(4,128)(2,1)}, u32[]{:S(2)}) copy-start(bf16[4,6144]{1,0:T(4,128)(2,1)} %param.11) | copy-start | bytes 147460
  52.6 86.0 %copy-start.2 = (f32[6144]{0:T(1024)S(1)}, f32[6144]{0:T(1024)}, u32[]{:S(2)}) copy-start(f32[6144]{0:T(1024)} %param.12) | copy-start | bytes 73732
  129.5 7.6 %all-to-all-start.2 = ((bf16[4,2,6144]{2,1,0:T(2,128)(2,1)}), bf16[4,2,6144]{2,1,0:T(2,128)(2,1)S(1)}, u32[]{:S(2)}, u32[]{:S(2)}) async-start(bf16[4,2,6144]{2,1,0:T(2,128)(2,1)} %all_to_all.37), calls=%async_computation.3 | async-start | bytes 196608 | tf_op jit(solution)/shard_map/all_to_all | solution.py:84
  132.8 119.1 %reduce-scatter.5.cloned.1.call-start = ((), (), s32[]{:S(2)}) async-start(), calls=%async_computation.9 | async-start | bytes 884736 | tf_op jit(solution)/shard_map/reduce_scatter | solution.py:81
Sparse Core Ops, SparseCore 0:
  66.3 61.4 reduce-scatter.2
  190.4 61.4 reduce-scatter.4
